TPU v7x, 32 devices: a whole 2x2x4 slice. The times are simulated.
32 devices in a mesh: job: 2 (over y), blk: 4 (over z), cell: 2 (over x), col: 2 (over core).
Axes of the slice: x: 2, y: 2, z: 4, core: 2. Of those that a mesh axis runs over, the one named last changes fastest.
Arguments:
- p_blocks: bfloat16 [64, 4, 2, 128, 128], P(('job', 'blk', 'cell')), parts along dimension 0, may hold values from -0.1875 to 0.1875
- p_cols: int32 [64, 4, 2], P(('job', 'blk', 'cell')), parts along dimension 0, may hold values from 0 to 7
- l_blocks: bfloat16 [64, 4, 2, 128, 128], P(('job', 'blk', 'cell')), parts along dimension 0, may hold values from -0.1875 to 0.1875
- l_cols: int32 [64, 4, 2], P(('job', 'blk', 'cell')), parts along dimension 0, may hold values from 0 to 7
- charges: bfloat16 [24, 2, 8192], P('col', None, ('job', 'blk', 'cell')), parts along dimension 2, may hold values from -6 to 6
- currents: bfloat16 [24, 2, 8192], P('col', None, ('job', 'blk', 'cell')), parts along dimension 2, may hold values from -6 to 6
- omegas: float32 [24], P('col'), may hold values from 0.5 to 4
- resist: float32 [8192], P(('job', 'blk', 'cell')), parts along dimension 0, may hold values from 0.05 to 2
- branch_ends: int32 [2, 8192], P(None, ('job', 'blk', 'cell')), parts along dimension 1, may hold values from 0 to 1023
Outputs:
- cell_rows: float32 [24, 2, 8192], P('col', None, ('job', 'blk', 'cell')), parts along dimension 2
- panel_rows: float32 [24, 2, 8192], P('col', None, ('job', 'blk', 'cell')), parts along dimension 2
There are 2 independent parts, one for each index of `job`. A program takes and returns all parts, laid end to end along the dimension named above; an argument that names none is the same for every part. Nothing has to cross between parts.
Inputs may be any that keep to these rules, and one draw needn't show every extreme that they name: `p_cols`: block columns are numbered within the region of 8 blocks that the slot's region index names; repeats may occur. `l_cols`: as for p_cols. `branch_ends`: panel numbers within the cell's own region of 1024 panels; a cell may leave and enter the same panel.
All inputs are finite; a program needn't handle non-finite values.
Results may differ from a plain program's by a relative error of at most 0.0059.
Values may be sent and summed in bfloat16 or wider, within the bound.
A program may use at most 64 MiB of HBM per device.

v0:
```python
import jax
import jax.numpy as jnp
from jax import lax
from jax.sharding import PartitionSpec as P


def passed_along(shard, axis, by):
    length = lax.axis_size(axis)
    return lax.ppermute(shard, axis, [(i, (i + by) % length) for i in range(length)])


def per_device(p_blocks, p_cols, l_blocks, l_cols, charges, currents, omegas, resist, branch_ends):
    freq_count = charges.shape[0]
    share = charges.shape[2]
    block_size = p_blocks.shape[-1]
    row_blocks = p_blocks.shape[0]
    col_rows = 2 * freq_count
    stacked = jnp.stack([charges.reshape(col_rows, share), currents.reshape(col_rows, share)])
    region_vec = lax.all_gather(stacked, "cell", axis=2, tiled=True)
    reg_width = region_vec.shape[2]
    reg_blocks = reg_width // block_size
    blk_count = lax.axis_size("blk")
    blk_place = lax.axis_index("blk")

    def accumulate(totals, whole, source):
        p_slab = lax.dynamic_index_in_dim(p_blocks, source, 1, keepdims=False)
        p_index = lax.dynamic_index_in_dim(p_cols, source, 1, keepdims=False)
        l_slab = lax.dynamic_index_in_dim(l_blocks, source, 1, keepdims=False)
        l_index = lax.dynamic_index_in_dim(l_cols, source, 1, keepdims=False)
        vectors = whole.reshape(2, col_rows, reg_blocks, block_size)
        q_picked = vectors[0][:, p_index]
        i_picked = vectors[1][:, l_index]
        phi_add = jnp.einsum("rkab,frkb->fra", p_slab, q_picked, preferred_element_type=jnp.float32)
        flux_add = jnp.einsum(
            "rkab,frkb->fra", l_slab, i_picked, preferred_element_type=jnp.float32
        )
        return (totals[0] + phi_add, totals[1] + flux_add)

    zeros_acc = jnp.zeros((col_rows, row_blocks, block_size), jnp.float32)
    totals = accumulate((zeros_acc, zeros_acc), region_vec, blk_place)

    def forward(offset, carry):
        acc, held = carry
        held = passed_along(held, "blk", 1)
        acc = accumulate(acc, held, (blk_place - offset - 1) % blk_count)
        return (acc, held)

    totals, held_last = lax.fori_loop(0, blk_count - 1, forward, (totals, region_vec))
    potential = totals[0].reshape(col_rows, share).astype(jnp.bfloat16)
    flux = totals[1].reshape(freq_count, 2, share)
    phi_region = lax.all_gather(potential, "cell", axis=1, tiled=True)
    drop = phi_region[:, branch_ends[0]].astype(jnp.float32) - phi_region[:, branch_ends[1]].astype(
        jnp.float32
    )
    drop = drop.reshape(freq_count, 2, share)
    current_f = currents.astype(jnp.float32)
    scale = omegas[:, None]
    cell_re = resist * current_f[:, 0] - scale * flux[:, 1] + drop[:, 0]
    cell_im = resist * current_f[:, 1] + scale * flux[:, 0] + drop[:, 1]
    cell_rows = jnp.stack([cell_re, cell_im], axis=1)
    panel_ids = jnp.arange(reg_width, dtype=jnp.int32)
    incidence = (branch_ends[0][:, None] == panel_ids[None, :]).astype(jnp.bfloat16) - (
        branch_ends[1][:, None] == panel_ids[None, :]
    ).astype(jnp.bfloat16)
    partial_terms = jnp.dot(
        currents.reshape(col_rows, share), incidence, preferred_element_type=jnp.float32
    )
    outflow = lax.psum_scatter(
        partial_terms.astype(jnp.bfloat16), "cell", scatter_dimension=1, tiled=True
    ).astype(jnp.float32)
    outflow = outflow.reshape(freq_count, 2, share)
    charge_f = charges.astype(jnp.float32)
    panel_re = outflow[:, 0] - scale * charge_f[:, 1]
    panel_im = outflow[:, 1] + scale * charge_f[:, 0]
    panel_rows = jnp.stack([panel_re, panel_im], axis=1)
    return (cell_rows, panel_rows)


def solution(mesh):
    placed = (
        P(("job", "blk", "cell"), None, None, None, None),
        P(("job", "blk", "cell"), None, None),
        P(("job", "blk", "cell"), None, None, None, None),
        P(("job", "blk", "cell"), None, None),
        P("col", None, ("job", "blk", "cell")),
        P("col", None, ("job", "blk", "cell")),
        P("col"),
        P(("job", "blk", "cell")),
        P(None, ("job", "blk", "cell")),
    )
    return jax.shard_map(
        per_device,
        mesh=mesh,
        in_specs=placed,
        out_specs=(P("col", None, ("job", "blk", "cell")), P("col", None, ("job", "blk", "cell"))),
        check_vma=False,
    )
```

profile of v0, /device:TPU:0, one launch (start us, length us, event | category | flops | bytes accessed | tf_op | source)
XLA Modules:
  0.0 61.0 jit_solution(2294230764357474805)
XLA Ops:
  7.3 0.8 %fusion.26 = (s32[1,512]{1,0:T(1,128)S(1)}, s32[1,512]{1,0:T(1,128)S(1)}) fusion(s32[2,512]{1,0:T(2,128)} %param.19), kind=kLoop, calls=%fused_computation.67 | loop fusion | bytes 8192 | tf_op jit(solution)/shard_map/slice | solution.py:52
  8.0 0.8 %reshape.253 = bf16[24,512]{1,0:T(8,128)(2,1)S(1)} reshape(bf16[12,2,512]{2,1,0:T(2,128)(2,1)} %param.16) | data formatting | bytes 49152 | tf_op jit(solution)/shard_map/reshape | solution.py:66
  8.8 1.3 %fusion.10 = bf16[24,1024]{1,0:T(8,128)(2,1)} fusion(bf16[24,512]{1,0:T(8,128)(2,1)S(1)} %reshape.253, s32[512]{0:T(512)S(1)} %bitcast.138, s32[512]{0:T(512)S(1)} %bitcast.137), kind=kOutput, calls=%fused_computation.27 | convolution fusion | flops 29384704 | bytes 77824 | tf_op jit(solution)/shard_map/dot_general | solution.py:65
  10.9 5.7 %all_gather.6 = bf16[2,24,1024]{2,1,0:T(8,128)(2,1)S(1)} all-gather(bf16[2,24,512]{2,1,0:T(8,128)(2,1)S(1)} %pad_maximum_fusion), channel_id=1, replica_groups=mesh['job'=2,'blk'=4,'cell'=2,'col'=2] {'cell'}, dimensions={2}, use_global_device_ids=true | all-gather | bytes 147456 | tf_op jit(solution)/shard_map/all_gather | solution.py:19
  16.9 0.6 gather_fusion.3
  17.6 0.6 gather_fusion.2
  18.4 24.6 %while.19 = (s32[]{:T(128)}, f32[24,4,128]{2,0,1:T(8,128)S(1)}, f32[24,4,128]{2,0,1:T(8,128)S(1)}, bf16[2,24,1024]{2,1,0:T(8,128)(2,1)S(1)}, s32[]{:T(128)}, /*i...) while((s32[]{:T(128)}, f32[24,4,128]{2,0,1:T(8,128)S(1)}, ...), condition=%wide.region_1.2_spmd, body=%wide.region_0.1_spmd.sunk | while | flops 12609602 | bytes 2204512 | solution.py:48
  18.4 2.2 %collective-permute-start = (bf16[2,24,1024]{2,1,0:T(8,128)(2,1)S(1)}, bf16[2,24,1024]{2,1,0:T(8,128)(2,1)S(1)}, u32[]{:S(2)}, u32[]{:S(2)}) collective-permute-start(bf16[2,24,1024]{2,1,0:T(8,128)(2,1)S(1)} %get-tuple-element.370), channel_id=1, source_target_pairs={{0,4},{4,8},{8,12},{12,0},{1,5},{5,9},{9,13},{13,1},{2,6},{6,10},{... | collective-permute-start | bytes 294920 | tf_op jit(solution)/shard_map/while/body/eval_jaxpr/ppermute | solution.py:9
  20.9 4.2 %collective-permute-done = bf16[2,24,1024]{2,1,0:T(8,128)(2,1)S(1)} collective-permute-done((bf16[2,24,1024]{2,1,0:T(8,128)(2,1)S(1)}, bf16[2,24,1024]{2,1,0:T(8,128)(2,1)S(1)}, u32[]{:S(2)}, u32[]{:S(2)}) %collective-permute-start) | collective-permute-done | bytes 98336 | tf_op jit(solution)/shard_map/while/body/eval_jaxpr/ppermute | solution.py:9
  25.2 0.6 gather_fusion.1
  25.8 0.6 gather_fusion
  27.3 6.0 %collective-permute-done = bf16[2,24,1024]{2,1,0:T(8,128)(2,1)S(1)} collective-permute-done((bf16[2,24,1024]{2,1,0:T(8,128)(2,1)S(1)}, bf16[2,24,1024]{2,1,0:T(8,128)(2,1)S(1)}, u32[]{:S(2)}, u32[]{:S(2)}) %collective-permute-start) | collective-permute-done | bytes 98336 | tf_op jit(solution)/shard_map/while/body/eval_jaxpr/ppermute | solution.py:9
  33.4 0.6 gather_fusion.1
  33.9 0.6 gather_fusion
  35.4 6.0 %collective-permute-done = bf16[2,24,1024]{2,1,0:T(8,128)(2,1)S(1)} collective-permute-done((bf16[2,24,1024]{2,1,0:T(8,128)(2,1)S(1)}, bf16[2,24,1024]{2,1,0:T(8,128)(2,1)S(1)}, u32[]{:S(2)}, u32[]{:S(2)}) %collective-permute-start) | collective-permute-done | bytes 98336 | tf_op jit(solution)/shard_map/while/body/eval_jaxpr/ppermute | solution.py:9
  41.5 0.6 gather_fusion.1
  42.0 0.6 gather_fusion
  43.2 5.6 %all_gather.7 = bf16[24,1024]{0,1:T(8,128)(2,1)S(1)} all-gather(bf16[24,512]{0,1:T(8,128)(2,1)S(1)} %bitcast.130), channel_id=1, replica_groups=mesh['job'=2,'blk'=4,'cell'=2,'col'=2] {'cell'}, dimensions={1}, use_global_device_ids=true | all-gather | bytes 73728 | tf_op jit(solution)/shard_map/all_gather | solution.py:51
  48.8 1.3 %gather_fusion.4 = bf16[512,24]{1,0:T(8,128)(2,1)S(1)} fusion(bf16[24,1024]{0,1:T(8,128)(2,1)S(1)} %all_gather.7, s32[1024]{0:T(1024)S(1)} %pad_clamp_fusion.3), kind=kCustom, calls=%fused_computation.4 | custom fusion | bytes 51200 | tf_op jit(solution)/shard_map/gather | solution.py:52
  50.2 1.3 %gather_fusion.5 = bf16[512,24]{1,0:T(8,128)(2,1)S(1)} fusion(bf16[24,1024]{0,1:T(8,128)(2,1)S(1)} %all_gather.7, s32[1024]{0:T(1024)S(1)} %pad_clamp_fusion.2), kind=kCustom, calls=%fused_computation.5 | custom fusion | bytes 51200 | tf_op jit(solution)/shard_map/gather | solution.py:52
  51.9 0.8 %reshape.257 = f32[12,2,512]{2,1,0:T(2,128)S(1)} reshape(bf16[24,512]{1,0:T(8,128)(2,1)} %reduce-scatter.2.cloned.1.call-done) | data formatting | bytes 73728 | tf_op jit(solution)/shard_map/reshape | solution.py:71
  52.7 0.2 fusion.21
  52.9 0.7 %pad_maximum_fusion.2 = f32[12,2,512]{2,1,0:T(2,128)} fusion(f32[12,1,512]{2,1,0:T(1,128)S(1)} %get-tuple-element.279, f32[12,1,512]{2,1,0:T(1,128)S(1)} %get-tuple-element.278), kind=kLoop, calls=%fused_computation.42 | loop fusion | flops 12288 | bytes 98304 | tf_op jit(solution)/shard_map/stack | solution.py:75
  53.5 0.7 %pad_maximum_fusion.1 = f32[12,2,512]{2,1,0:T(2,128)} fusion(f32[12,1,512]{2,1,0:T(1,128)S(1)} %get-tuple-element.286, f32[12,1,512]{2,1,0:T(1,128)S(1)} %get-tuple-element.287), kind=kLoop, calls=%fused_computation.41 | loop fusion | flops 12288 | bytes 98304 | tf_op jit(solution)/shard_map/stack | solution.py:60
  (103 shorter events, 4.5 us)
Async XLA Ops:
  7.2 3.3 %copy-start.6 = (s32[2,512]{1,0:T(2,128)S(1)}, s32[2,512]{1,0:T(2,128)}, u32[]{:S(2)}) copy-start(s32[2,512]{1,0:T(2,128)} %param.19) | copy-start | bytes 12292
  7.2 2.9 %copy-start.2 = (bf16[12,2,512]{2,1,0:T(2,128)(2,1)S(1)}, bf16[12,2,512]{2,1,0:T(2,128)(2,1)}, u32[]{:S(2)}) copy-start(bf16[12,2,512]{2,1,0:T(2,128)(2,1)} %param.16) | copy-start | bytes 73732
  7.2 3.0 %copy-start.4 = (s32[4,4,2]{1,2,0:T(2,128)S(1)}, s32[4,4,2]{1,2,0:T(2,128)}, u32[]{:S(2)}) copy-start(s32[4,4,2]{1,2,0:T(2,128)} %param.12) | copy-start | bytes 388
  7.2 3.1 %copy-start.5 = (s32[4,4,2]{1,2,0:T(2,128)S(1)}, s32[4,4,2]{1,2,0:T(2,128)}, u32[]{:S(2)}) copy-start(s32[4,4,2]{1,2,0:T(2,128)} %param.14) | copy-start | bytes 388
  7.2 44.7 %reduce-scatter.2.cloned.1.call-start = ((), (), s32[]{:S(2)}) async-start(), calls=%async_computation.1 | async-start | bytes 73728 | tf_op jit(solution)/shard_map/reduce_scatter | solution.py:68
  8.0 2.9 %copy-start.3 = (bf16[12,2,512]{2,1,0:T(2,128)(2,1)S(1)}, bf16[12,2,512]{2,1,0:T(2,128)(2,1)}, u32[]{:S(2)}) copy-start(bf16[12,2,512]{2,1,0:T(2,128)(2,1)} %param.15) | copy-start | bytes 73732
  8.8 8.7 %copy-start.1 = (bf16[4,4,2,128,128]{4,3,2,1,0:T(8,128)(2,1)S(1)}, bf16[4,4,2,128,128]{4,3,2,1,0:T(8,128)(2,1)}, u32[]{:S(2)}) copy-start(bf16[4,4,2,128,128]{4,3,2,1,0:T(8,128)(2,1)} %param.13) | copy-start | bytes 3145732
  10.1 8.1 %copy-start = (bf16[4,4,2,128,128]{4,3,2,1,0:T(8,128)(2,1)S(1)}, bf16[4,4,2,128,128]{4,3,2,1,0:T(8,128)(2,1)}, u32[]{:S(2)}) copy-start(bf16[4,4,2,128,128]{4,3,2,1,0:T(8,128)(2,1)} %param.11) | copy-start | bytes 3145732
  18.4 6.8 %collective-permute-start = (bf16[2,24,1024]{2,1,0:T(8,128)(2,1)S(1)}, bf16[2,24,1024]{2,1,0:T(8,128)(2,1)S(1)}, u32[]{:S(2)}, u32[]{:S(2)}) collective-permute-start(bf16[2,24,1024]{2,1,0:T(8,128)(2,1)S(1)} %get-tuple-element.370), channel_id=1, source_target_pairs={{0,4},{4,8},{8,12},{12,0},{1,5},{5,9},{9,13},{13,1},{2,6},{6,10},{... | collective-permute-start | bytes 294920 | tf_op jit(solution)/shard_map/while/body/eval_jaxpr/ppermute | solution.py:9
  26.8 6.5 %collective-permute-start = (bf16[2,24,1024]{2,1,0:T(8,128)(2,1)S(1)}, bf16[2,24,1024]{2,1,0:T(8,128)(2,1)S(1)}, u32[]{:S(2)}, u32[]{:S(2)}) collective-permute-start(bf16[2,24,1024]{2,1,0:T(8,128)(2,1)S(1)} %get-tuple-element.370), channel_id=1, source_target_pairs={{0,4},{4,8},{8,12},{12,0},{1,5},{5,9},{9,13},{13,1},{2,6},{6,10},{... | collective-permute-start | bytes 294920 | tf_op jit(solution)/shard_map/while/body/eval_jaxpr/ppermute | solution.py:9
  34.9 6.5 %collective-permute-start = (bf16[2,24,1024]{2,1,0:T(8,128)(2,1)S(1)}, bf16[2,24,1024]{2,1,0:T(8,128)(2,1)S(1)}, u32[]{:S(2)}, u32[]{:S(2)}) collective-permute-start(bf16[2,24,1024]{2,1,0:T(8,128)(2,1)S(1)} %get-tuple-element.370), channel_id=1, source_target_pairs={{0,4},{4,8},{8,12},{12,0},{1,5},{5,9},{9,13},{13,1},{2,6},{6,10},{... | collective-permute-start | bytes 294920 | tf_op jit(solution)/shard_map/while/body/eval_jaxpr/ppermute | solution.py:9
  43.2 9.5 %copy-start.7 = (f32[512]{0:T(512)S(1)}, f32[512]{0:T(512)}, u32[]{:S(2)}) copy-start(f32[512]{0:T(512)} %param.18) | copy-start | bytes 6148
  43.2 9.5 %copy-start.8 = (f32[12]{0:T(128)S(1)}, f32[12]{0:T(128)}, u32[]{:S(2)}) copy-start(f32[12]{0:T(128)} %param.17) | copy-start | bytes 148
Sparse Core Ops, SparseCore 0:
  10.8 12.5 reduce-scatter.1
where the time goes:
time: 61.4 us; the launch traced here: 61 us
  waiting for transfers between devices  16.2 us (26%)
  between operations  14.3 us (23%)
  local copies, waits for them, and re-layouts  12.1 us (20%)
  blocking collectives  11.3 us (18%)
  matrix products  2.73 us (4%)
  starting transfers between devices  2.31 us (4%)
  other arithmetic  1.74 us (3%)
    ppermute x3, waiting for transfers between devices, passed_along(): lax.ppermute(shard, axis, [(i, (i + by) % length) for i in range(length)])  16.2 us
    all_gather x1, blocking collectives, per_device(): region_vec = lax.all_gather(stacked, 'cell', axis=2, tiled=True)  5.66 us
    all_gather x1, blocking collectives, per_device(): phi_region = lax.all_gather(potential, 'cell', axis=1, tiled=True)  5.64 us
    gather x4, local copies, waits for them, and re-layouts, accumulate(): q_picked = vectors[0][:, p_index]  2.28 us
    ppermute x3, starting transfers between devices, passed_along(): lax.ppermute(shard, axis, [(i, (i + by) % length) for i in range(length)])  2.27 us
    gather x4, local copies, waits for them, and re-layouts, accumulate(): i_picked = vectors[1][:, l_index]  2.26 us
    gather x1, local copies, waits for them, and re-layouts, per_device(): phi_region[:, branch_ends[0]].astype(jnp.float32)  1.34 us
    gather x1, local copies, waits for them, and re-layouts, per_device(): phi_region[:, branch_ends[1]].astype(jnp.float32)  1.34 us
  transfers between devices with their start and end apart: 4, of which 3 were waited for; matrix products, arithmetic and copies ran while one was open for 19% of the time, Pallas kernels for 0%

commit v1 on v0

v1 whole, which is shorter than its diff:
```python
import functools

import jax
import jax.numpy as jnp
from jax import lax
from jax.experimental import pallas as pl
from jax.experimental.pallas import tpu as pltpu
from jax.sharding import PartitionSpec as P

MESH = pl.DeviceIdType.MESH
NT = (((1,), (1,)), ((), ()))
NN = (((1,), (0,)), ((), ()))


def dot(a, b, dims):
    return lax.dot_general(a, b, dims, preferred_element_type=jnp.float32)


def quarter_turn(x):
    rows = x.shape[0]
    even = lax.broadcasted_iota(jnp.int32, x.shape, 0) % 2 == 0
    return jnp.where(even, -pltpu.roll(x, rows - 1, 0), pltpu.roll(x, 1, 0))


def kernel(n_blk, n_cell, p_cols, l_cols, omegas, resist, ends, charges, currents, p_hbm, l_hbm,
           cell_out, panel_out, *scratch):
    a_bufs, b_bufs = scratch[:n_blk], scratch[n_blk : 2 * n_blk]
    (p_buf, l_buf, inc, phi, part_out, part_in, load_sem, a_send, a_recv, b_send, b_recv,
     phi_send, phi_recv, part_send, part_recv) = scratch[2 * n_blk :]
    rows, share = charges.shape
    local = share // 128
    my_blk, my_cell = lax.axis_index("blk"), lax.axis_index("cell")

    p_load = pltpu.make_async_copy(p_hbm, p_buf, load_sem.at[0])
    l_load = pltpu.make_async_copy(l_hbm, l_buf, load_sem.at[1])
    p_load.start()
    l_load.start()

    barrier = pltpu.get_barrier_semaphore()
    for d in range(1, n_blk):
        pl.semaphore_signal(barrier, device_id={"blk": lax.rem(my_blk + d, n_blk)}, device_id_type=MESH)
    for c in range(1, n_cell):
        pl.semaphore_signal(barrier, device_id={"cell": lax.rem(my_cell + c, n_cell)}, device_id_type=MESH)

    q32 = charges[...].astype(jnp.float32)
    i32 = currents[...].astype(jnp.float32)
    i16 = currents[...]
    mixed = jnp.concatenate([q32, i32[16:]], axis=0).astype(jnp.bfloat16)
    mine = pl.ds(my_cell * local, local)
    for b in range(local):
        cols = slice(b * 128, (b + 1) * 128)
        a_bufs[0][my_cell * local + b] = mixed[:, cols]
        b_bufs[0][my_cell * local + b] = i16[:16, cols]

    pl.semaphore_wait(barrier, n_blk - 1 + n_cell - 1)

    def along_blk(bufs, send, recv, d):
        return pltpu.make_async_remote_copy(
            src_ref=bufs[0].at[mine], dst_ref=bufs[d].at[mine],
            send_sem=send.at[d, 0], recv_sem=recv.at[d, 0],
            device_id={"blk": lax.rem(my_blk + d, n_blk)}, device_id_type=MESH)

    def along_cell(bufs, send, recv, d, c):
        return pltpu.make_async_remote_copy(
            src_ref=bufs[d].at[mine], dst_ref=bufs[d].at[mine],
            send_sem=send.at[d, c], recv_sem=recv.at[d, c],
            device_id={"cell": lax.rem(my_cell + c, n_cell)}, device_id_type=MESH)

    order = sorted(range(1, n_blk), key=lambda d: min(d, n_blk - d))
    hops = range(1, n_cell)
    a_set, b_set = (a_bufs, a_send, a_recv), (b_bufs, b_send, b_recv)
    for group in (a_set, b_set):
        for d in order[::-1]:
            along_blk(*group, d).start()
        for c in hops:
            along_cell(*group, 0, c).start()

    start = ends[0:1, :]
    stop = ends[1:2, :]
    chunk = 128
    base = lax.broadcasted_iota(jnp.int32, (chunk, share), 0)

    def fill(t, carry):
        offset = pl.multiple_of(t * chunk, chunk)
        plus = jnp.where(base == start - offset, 1.0, 0.0)
        minus = jnp.where(base == stop - offset, 1.0, 0.0)
        inc[pl.ds(offset, chunk), :] = (plus - minus).astype(jnp.bfloat16)
        return carry

    lax.fori_loop(0, n_cell * share // chunk, fill, 0)

    def inc_of(owner):
        return inc[pl.ds(pl.multiple_of(owner * share, share), share), :]

    def part_copy(c):
        return pltpu.make_async_remote_copy(
            src_ref=part_out.at[c], dst_ref=part_in.at[c],
            send_sem=part_send.at[c], recv_sem=part_recv.at[c],
            device_id={"cell": lax.rem(my_cell + c, n_cell)}, device_id_type=MESH)

    for c in hops:
        owner = lax.rem(my_cell + c, n_cell)
        part_out[c] = dot(i16, inc_of(owner), NT).astype(jnp.bfloat16)
        part_copy(c).start()

    for d in order:
        along_blk(*a_set, d).wait_recv()
        for c in hops:
            along_cell(*a_set, d, c).start()

    outflow = dot(i16, inc_of(my_cell), NT)
    row = lax.broadcasted_iota(jnp.int32, (rows, 128), 0) // 2
    omega = jnp.zeros((rows, 128), jnp.float32)
    for f in range(rows // 2):
        omega = jnp.where(row == f, omegas[f], omega)
    omega = jnp.concatenate([omega] * local, axis=1)

    def add_products(acc, blocks, cols, d, pick):
        source = lax.rem(my_blk + n_blk - d, n_blk)
        for r in range(local):
            left = jnp.concatenate([pick(d, cols[r, source, k]) for k in range(2)], axis=1)
            right = jnp.concatenate([blocks[r, source, k] for k in range(2)], axis=1)
            term = dot(left, right, NT)
            acc[r] = term if acc[r] is None else acc[r] + term

    def pick_q(d, j):
        return a_bufs[d][j]

    def pick_i(d, j):
        return jnp.concatenate([b_bufs[d][j], a_bufs[d][j, 16:]], axis=0)

    for c in hops:
        along_cell(*a_set, 0, c).wait_recv()
    p_load.wait()
    acc = [None] * local
    add_products(acc, p_buf, p_cols, 0, pick_q)

    for d in order:
        along_blk(*b_set, d).wait_recv()
        for c in hops:
            along_cell(*b_set, d, c).start()
    for d in order:
        for c in hops:
            along_cell(*a_set, d, c).wait_recv()
        add_products(acc, p_buf, p_cols, d, pick_q)

    phi[0] = jnp.concatenate(acc, axis=1).astype(jnp.bfloat16)

    def phi_copy(c):
        return pltpu.make_async_remote_copy(
            src_ref=phi.at[0], dst_ref=phi.at[c],
            send_sem=phi_send.at[c], recv_sem=phi_recv.at[c],
            device_id={"cell": lax.rem(my_cell + c, n_cell)}, device_id_type=MESH)

    for c in hops:
        phi_copy(c).start()

    for c in hops:
        along_cell(*b_set, 0, c).wait_recv()
    l_load.wait()
    acc = [None] * local
    add_products(acc, l_buf, l_cols, 0, pick_i)
    for d in order:
        for c in hops:
            along_cell(*b_set, d, c).wait_recv()
        add_products(acc, l_buf, l_cols, d, pick_i)
    flux = jnp.concatenate(acc, axis=1)
    flux = jnp.concatenate([flux[:16], flux[24:]], axis=0)
    cell = resist[...] * i32 + omega * quarter_turn(flux)
    drop = dot(phi[0], inc_of(my_cell), NN)

    for c in hops:
        part_copy(c).wait_recv()
        outflow += part_in[c].astype(jnp.float32)
    panel_out[...] = outflow + omega * quarter_turn(q32)

    for c in hops:
        phi_copy(c).wait_recv()
        drop += dot(phi[c], inc_of(lax.rem(my_cell + n_cell - c, n_cell)), NN)
    cell_out[...] = cell + drop[:rows]

    for c in hops:
        part_copy(c).wait_send()
        phi_copy(c).wait_send()
    for group in (a_set, b_set):
        for d in order:
            along_blk(*group, d).wait_send()
        for d in range(n_blk):
            for c in hops:
                along_cell(*group, d, c).wait_send()


def per_device(p_blocks, p_cols, l_blocks, l_cols, charges, currents, omegas, resist, branch_ends):
    n_blk, n_cell = lax.axis_size("blk"), lax.axis_size("cell")
    freq_count, _, share = charges.shape
    rows = 2 * freq_count
    reg_blocks = n_cell * share // 128
    vmem = pl.BlockSpec(memory_space=pltpu.VMEM)
    smem = pl.BlockSpec(memory_space=pltpu.SMEM)
    hbm = pl.BlockSpec(memory_space=pltpu.HBM)
    dma = pltpu.SemaphoreType.DMA
    outs = pl.pallas_call(
        functools.partial(kernel, n_blk, n_cell),
        out_shape=[jax.ShapeDtypeStruct((rows, share), jnp.float32)] * 2,
        in_specs=[smem, smem, smem, vmem, vmem, vmem, vmem, hbm, hbm],
        out_specs=[vmem, vmem],
        scratch_shapes=[pltpu.VMEM((reg_blocks, 32, 128), jnp.bfloat16)] * n_blk
        + [pltpu.VMEM((reg_blocks, 16, 128), jnp.bfloat16)] * n_blk
        + [
            pltpu.VMEM(p_blocks.shape, p_blocks.dtype),
            pltpu.VMEM(l_blocks.shape, l_blocks.dtype),
            pltpu.VMEM((n_cell * share, share), jnp.bfloat16),
            pltpu.VMEM((n_cell, 32, share), jnp.bfloat16),
            pltpu.VMEM((n_cell, rows, share), jnp.bfloat16),
            pltpu.VMEM((n_cell, rows, share), jnp.bfloat16),
            dma((2,)),
            dma((n_blk, n_cell)), dma((n_blk, n_cell)),
            dma((n_blk, n_cell)), dma((n_blk, n_cell)),
            dma((n_cell,)), dma((n_cell,)),
            dma((n_cell,)), dma((n_cell,)),
        ],
        compiler_params=pltpu.CompilerParams(
            collective_id=0, has_side_effects=True, vmem_limit_bytes=40 * 2**20
        ),
    )(
        p_cols, l_cols, omegas, resist.reshape(1, share), branch_ends,
        charges.reshape(rows, share), currents.reshape(rows, share), p_blocks, l_blocks,
    )
    return tuple(o.reshape(freq_count, 2, share) for o in outs)


def solution(mesh):
    across = ("job", "blk", "cell")
    placed = (
        P(across, None, None, None, None),
        P(across, None, None),
        P(across, None, None, None, None),
        P(across, None, None),
        P("col", None, across),
        P("col", None, across),
        P("col"),
        P(across),
        P(None, across),
    )
    return jax.shard_map(
        per_device,
        mesh=mesh,
        in_specs=placed,
        out_specs=(P("col", None, across), P("col", None, across)),
        check_vma=False,
    )
```

time: 61.4 us -> 26.1 us (0.43)
  Pallas kernels: 0 us -> 18.3 us
  waiting for transfers between devices: 16.2 us -> 0 us
  between operations: 14.3 us -> 0.66 us
  blocking collectives: 11.3 us -> 0 us
  local copies, waits for them, and re-layouts: 12.1 us -> 6.77 us
  matrix products: 2.73 us -> 0 us
  starting transfers between devices: 2.31 us -> 0 us
  other arithmetic: 1.74 us -> 0 us
    pallas_call x0 -> x1, Pallas kernels: none -> 18.3 us  [per_device(): pl.pallas_call(functools.partial(kernel, n_blk, n_cell), out_shape=[jax.S...]
    ppermute x3 -> x0, waiting for transfers between devices: 16.2 us -> none  [passed_along(): lax.ppermute(shard, axis, [(i, (i + by) % length) for i in range(length)])]
    all_gather x2 -> x0, blocking collectives: 11.3 us -> none  [the longest x1 5.66 us: per_device(): region_vec = lax.all_gather(stacked, 'cell', axis=2, tiled=True)]
    gather x10 -> x0, local copies, waits for them, and re-layouts: 7.23 us -> none  [the longest x4 2.28 us: accumulate(): q_picked = vectors[0][:, p_index]]
    unnamed x21 -> x16, local copies, waits for them, and re-layouts: 0.07 us -> 5.44 us
    dot_general x9 -> x0, matrix products: 2.73 us -> none  [the longest x1 1.27 us: per_device(): jnp.dot(currents.reshape(col_rows, share), incidence, preferred_element_t...]
    ppermute x3 -> x0, starting transfers between devices: 2.27 us -> none  [passed_along(): lax.ppermute(shard, axis, [(i, (i + by) % length) for i in range(length)])]
    select_n x16 -> x0, local copies, waits for them, and re-layouts: 1.43 us -> none  [the longest x8 0.72 us: accumulate(): i_picked = vectors[1][:, l_index]]
  transfers between devices with their start and end apart: 4 -> 0, of which waited for: 3 -> 0; matrix products, arithmetic and copies ran while one was open for 19% -> 0% of each run, Pallas kernels for 0% -> 0%
where the time goes in v1:
time: 26.1 us; the launch traced here: 25.8 us
  Pallas kernels  18.3 us (70%)
  local copies, waits for them, and re-layouts  6.77 us (26%)
  between operations  0.66 us (3%)
    pallas_call x1, Pallas kernels, per_device(): pl.pallas_call(functools.partial(kernel, n_blk, n_cell), out_shape=[jax.S...  18.3 us
    unnamed x16, local copies, waits for them, and re-layouts  5.44 us
    reshape x2, local copies, waits for them, and re-layouts, per_device(): return tuple((o.reshape(freq_count, 2, share) for o in outs))  1.3 us

profile of v1, /device:TPU:0, one launch (start us, length us, event | category | flops | bytes accessed | tf_op | source)
XLA Modules:
  0.0 25.8 jit_solution(12619169101978976684)
XLA Ops:
  0.6 0.0 copy-start.5
  0.6 0.8 %copy.11.p_cols = s32[4,4,2]{2,1,0:T(4,128)S(1)} copy(s32[4,4,2]{1,2,0:T(2,128)} %param.10) | data formatting | bytes 256 | tf_op args[1]
  1.4 0.8 %copy.12.l_cols = s32[4,4,2]{2,1,0:T(4,128)S(1)} copy(s32[4,4,2]{1,2,0:T(2,128)} %param.12) | data formatting | bytes 256 | tf_op args[3]
  2.2 0.0 copy-done.5
  2.2 0.0 copy-start.6
  2.2 0.7 %copy-done.6 = bf16[12,2,512]{2,1,0:T(2,128)(2,1)S(1)} copy-done((bf16[12,2,512]{2,1,0:T(2,128)(2,1)S(1)}, bf16[12,2,512]{2,1,0:T(2,128)(2,1)}, u32[]{:S(2)}) %copy-start.6) | copy-done | bytes 24600
  3.0 0.0 copy-start.2
  3.0 0.0 copy-start.3
  3.0 0.0 copy-start.4
  3.0 0.7 %copy-done.2 = s32[2,512]{1,0:T(2,128)S(1)} copy-done((s32[2,512]{1,0:T(2,128)S(1)}, s32[2,512]{1,0:T(2,128)}, u32[]{:S(2)}) %copy-start.2) | copy-done | bytes 4120
  3.7 0.0 copy-done.3
  3.7 0.0 copy-done.4
  3.7 0.0 copy-start
  3.7 1.2 %copy-done = bf16[4,4,2,128,128]{4,3,2,1,0:T(8,128)(2,1)S(1)} copy-done((bf16[4,4,2,128,128]{4,3,2,1,0:T(8,128)(2,1)S(1)}, bf16[4,4,2,128,128]{4,3,2,1,0:T(8,128)(2,1)}, u32[]{:S(2)}) %copy-start) | copy-done | bytes 1048600
  4.9 0.0 copy-start.1
  4.9 1.2 %copy-done.1 = bf16[4,4,2,128,128]{4,3,2,1,0:T(8,128)(2,1)S(1)} copy-done((bf16[4,4,2,128,128]{4,3,2,1,0:T(8,128)(2,1)S(1)}, bf16[4,4,2,128,128]{4,3,2,1,0:T(8,128)(2,1)}, u32[]{:S(2)}) %copy-start.1) | copy-done | bytes 1048600
  6.1 18.3 %shard_map.104 = (f32[24,512]{1,0:T(8,128)S(1)}, f32[24,512]{1,0:T(8,128)S(1)}) custom-call(s32[4,4,2]{2,1,0:T(4,128)S(1)} %copy.11.p_cols, s32[4,4,2]{2,1,0:T(4,128)S(1)} %copy.12.l_cols, f32[12]{0:T(128)S(1)} %copy-done.4, f32[1,512]{1,0:T(1,128)S(1)} %bitcast.1, s32[2,512]{1,0:T(2,128)S(1)} %copy-done.2, bf16[24,512]{1,0:T(8,128)(2,1)S(1)} %reshape.20.charges, ...), custom_call_target="tpu_custom_call" | custom-call | tf_op jit(solution)/shard_map/pallas_call | solution.py:202
  24.5 0.6 %reshape.22 = f32[12,2,512]{2,1,0:T(2,128)} reshape(f32[24,512]{1,0:T(8,128)S(1)} %get-tuple-element.4) | data formatting | bytes 98304 | tf_op jit(solution)/shard_map/reshape | solution.py:229
  25.1 0.6 %reshape.23 = f32[12,2,512]{2,1,0:T(2,128)} reshape(f32[24,512]{1,0:T(8,128)S(1)} %get-tuple-element.5) | data formatting | bytes 98304 | tf_op jit(solution)/shard_map/reshape | solution.py:229
  (2 shorter events, 0.0 us)
Async XLA Ops:
  0.6 1.6 %copy-start.5 = (bf16[12,2,512]{2,1,0:T(2,128)(2,1)S(1)}, bf16[12,2,512]{2,1,0:T(2,128)(2,1)}, u32[]{:S(2)}) copy-start(bf16[12,2,512]{2,1,0:T(2,128)(2,1)} %param.13) | copy-start | bytes 73732
  2.2 0.7 %copy-start.6 = (bf16[12,2,512]{2,1,0:T(2,128)(2,1)S(1)}, bf16[12,2,512]{2,1,0:T(2,128)(2,1)}, u32[]{:S(2)}) copy-start(bf16[12,2,512]{2,1,0:T(2,128)(2,1)} %param.14) | copy-start | bytes 73732
  3.0 0.7 %copy-start.2 = (s32[2,512]{1,0:T(2,128)S(1)}, s32[2,512]{1,0:T(2,128)}, u32[]{:S(2)}) copy-start(s32[2,512]{1,0:T(2,128)} %ends.1) | copy-start | bytes 12292
  3.0 0.7 %copy-start.3 = (f32[512]{0:T(512)S(1)}, f32[512]{0:T(512)}, u32[]{:S(2)}) copy-start(f32[512]{0:T(512)} %param.16) | copy-start | bytes 6148
  3.0 0.7 %copy-start.4 = (f32[12]{0:T(128)S(1)}, f32[12]{0:T(128)}, u32[]{:S(2)}) copy-start(f32[12]{0:T(128)} %omegas.1) | copy-start | bytes 148
  3.7 1.2 %copy-start = (bf16[4,4,2,128,128]{4,3,2,1,0:T(8,128)(2,1)S(1)}, bf16[4,4,2,128,128]{4,3,2,1,0:T(8,128)(2,1)}, u32[]{:S(2)}) copy-start(bf16[4,4,2,128,128]{4,3,2,1,0:T(8,128)(2,1)} %p_hbm.1) | copy-start | bytes 3145732
  4.9 1.2 %copy-start.1 = (bf16[4,4,2,128,128]{4,3,2,1,0:T(8,128)(2,1)S(1)}, bf16[4,4,2,128,128]{4,3,2,1,0:T(8,128)(2,1)}, u32[]{:S(2)}) copy-start(bf16[4,4,2,128,128]{4,3,2,1,0:T(8,128)(2,1)} %l_hbm.1) | copy-start | bytes 3145732

commit v2 on v1

v2 whole, which is shorter than its diff:
```python
import functools

import jax
import jax.numpy as jnp
from jax import lax
from jax.experimental import pallas as pl
from jax.experimental.pallas import tpu as pltpu
from jax.sharding import PartitionSpec as P

MESH = pl.DeviceIdType.MESH
NT = (((1,), (1,)), ((), ()))
NN = (((1,), (0,)), ((), ()))


def dot(a, b, dims):
    return lax.dot_general(a, b, dims, preferred_element_type=jnp.float32)


def quarter_turn(x):
    rows = x.shape[0]
    even = lax.broadcasted_iota(jnp.int32, x.shape, 0) % 2 == 0
    return jnp.where(even, -pltpu.roll(x, rows - 1, 0), pltpu.roll(x, 1, 0))


def kernel(n_blk, n_cell, *refs):
    sources, both, scratch = refs[:9], refs[9], refs[10:]
    cell_out, panel_out = both.at[0], both.at[1]
    a_bufs, b_bufs = scratch[:n_blk], scratch[n_blk : 2 * n_blk]
    targets = scratch[2 * n_blk : 2 * n_blk + 9]
    charges, currents, ends, resist, omegas, p_cols, l_cols, p_buf, l_buf = targets
    (inc, phi, part_out, part_in, load_sem, a_send, a_recv, b_send, b_recv,
     phi_send, phi_recv, part_send, part_recv) = scratch[2 * n_blk + 9 :]
    rows, share = 2 * charges.shape[0], charges.shape[2]
    local = share // 128
    my_blk, my_cell = lax.axis_index("blk"), lax.axis_index("cell")

    barrier = pltpu.get_barrier_semaphore()
    peers = [(d, c) for d in range(n_blk) for c in range(n_cell) if (d or c) and not (d and c)]

    def device(d, c):
        return {"blk": lax.rem(my_blk + d, n_blk), "cell": lax.rem(my_cell + c, n_cell)}

    for d, c in peers:
        pl.semaphore_signal(barrier, device_id=device(d, c), device_id_type=MESH)

    loads = [
        pltpu.make_async_copy(src, dst, load_sem.at[i])
        for i, (src, dst) in enumerate(zip(sources, targets))
    ]
    for load in loads[:2]:
        load.start()

    for load in loads[:2]:
        load.wait()
    q32 = charges[...].astype(jnp.float32).reshape(rows, share)
    i32 = currents[...].astype(jnp.float32).reshape(rows, share)
    q16 = q32.astype(jnp.bfloat16)
    i16 = i32.astype(jnp.bfloat16)
    mine = pl.ds(my_cell * local, local)
    for b in range(local):
        cols = slice(b * 128, (b + 1) * 128)
        a_bufs[0][my_cell * local + b] = q16[:, cols]
        b_bufs[0][my_cell * local + b] = i16[:, cols]

    pl.semaphore_wait(barrier, len(peers))

    def send(group, d, c, straight):
        bufs, sent, landed = group
        source, to = (bufs[0], device(d, c)) if straight else (bufs[d], device(0, c))
        return pltpu.make_async_remote_copy(
            src_ref=source.at[mine], dst_ref=bufs[d].at[mine],
            send_sem=sent.at[d, c], recv_sem=landed.at[d, c],
            device_id=to, device_id_type=MESH)

    def along_blk(group, d):
        return send(group, d, 0, True)

    def along_cell(group, d, c):
        return send(group, d, c, False)

    order = sorted(range(1, n_blk), key=lambda d: min(d, n_blk - d))
    hops = range(1, n_cell)
    a_set, b_set = (a_bufs, a_send, a_recv), (b_bufs, b_send, b_recv)
    for group in (a_set, b_set):
        for d in order[::-1]:
            along_blk(group, d).start()
        for c in hops:
            along_cell(group, 0, c).start()
    for load in loads[2:]:
        load.start()

    for load in loads[2:7]:
        load.wait()
    start = ends[0:1, :]
    stop = ends[1:2, :]
    chunk = 128
    base = lax.broadcasted_iota(jnp.int32, (chunk, share), 0)

    def fill(t, carry):
        offset = pl.multiple_of(t * chunk, chunk)
        plus = jnp.where(base == start - offset, 1.0, 0.0)
        minus = jnp.where(base == stop - offset, 1.0, 0.0)
        inc[pl.ds(offset, chunk), :] = (plus - minus).astype(jnp.bfloat16)
        return carry

    lax.fori_loop(0, n_cell * share // chunk, fill, 0)

    def inc_of(owner):
        return inc[pl.ds(pl.multiple_of(owner * share, share), share), :]

    def part_copy(c):
        return pltpu.make_async_remote_copy(
            src_ref=part_out.at[c], dst_ref=part_in.at[c],
            send_sem=part_send.at[c], recv_sem=part_recv.at[c],
            device_id={"cell": lax.rem(my_cell + c, n_cell)}, device_id_type=MESH)

    for c in hops:
        owner = lax.rem(my_cell + c, n_cell)
        part_out[c] = dot(i16, inc_of(owner), NT).astype(jnp.bfloat16)

    def pass_on(group):
        for d in order:
            along_blk(group, d).wait_recv()
            for c in hops:
                along_cell(group, d, c).start()

    pass_on(a_set)

    outflow = dot(i16, inc_of(my_cell), NT)
    row = lax.broadcasted_iota(jnp.int32, (rows, 128), 0) // 2
    omega = jnp.zeros((rows, 128), jnp.float32)
    for f in range(rows // 2):
        omega = jnp.where(row == f, omegas[f], omega)
    omega = jnp.concatenate([omega] * local, axis=1)

    def add_products(acc, blocks, cols, d, pick):
        source = lax.rem(my_blk + n_blk - d, n_blk)
        for r in range(local):
            left = jnp.concatenate([pick(d, cols[r, k, source]) for k in range(2)], axis=1)
            right = jnp.concatenate([blocks[r, source, k] for k in range(2)], axis=1)
            term = dot(left, right, NT)
            acc[r] = term if acc[r] is None else acc[r] + term

    def pick_q(d, j):
        return a_bufs[d][j]

    def pick_i(d, j):
        return b_bufs[d][j]

    for c in hops:
        along_cell(a_set, 0, c).wait_recv()
    loads[7].wait()
    acc = [None] * local
    add_products(acc, p_buf, p_cols, 0, pick_q)

    pass_on(b_set)
    for d in order:
        for c in hops:
            along_cell(a_set, d, c).wait_recv()
        add_products(acc, p_buf, p_cols, d, pick_q)

    phi[0] = jnp.concatenate(acc, axis=1).astype(jnp.bfloat16)

    def phi_copy(c):
        return pltpu.make_async_remote_copy(
            src_ref=phi.at[0], dst_ref=phi.at[c],
            send_sem=phi_send.at[c], recv_sem=phi_recv.at[c],
            device_id={"cell": lax.rem(my_cell + c, n_cell)}, device_id_type=MESH)

    for c in hops:
        phi_copy(c).start()
    for c in hops:
        part_copy(c).start()

    for c in hops:
        along_cell(b_set, 0, c).wait_recv()
    loads[8].wait()
    acc = [None] * local
    add_products(acc, l_buf, l_cols, 0, pick_i)
    for d in order:
        for c in hops:
            along_cell(b_set, d, c).wait_recv()
        add_products(acc, l_buf, l_cols, d, pick_i)
    flux = jnp.concatenate(acc, axis=1)
    cell = resist[...] * i32 + omega * quarter_turn(flux)
    drop = dot(phi[0], inc_of(my_cell), NN)

    for c in hops:
        part_copy(c).wait_recv()
        outflow += part_in[c].astype(jnp.float32)
    panel_out[...] = (outflow + omega * quarter_turn(q32)).reshape(panel_out.shape)

    for c in hops:
        phi_copy(c).wait_recv()
        drop += dot(phi[c], inc_of(lax.rem(my_cell + n_cell - c, n_cell)), NN)
    cell_out[...] = (cell + drop).reshape(cell_out.shape)

    for c in hops:
        part_copy(c).wait_send()
        phi_copy(c).wait_send()
    for group in (a_set, b_set):
        for d in order:
            along_blk(group, d).wait_send()
        for d in range(n_blk):
            for c in hops:
                along_cell(group, d, c).wait_send()


def per_device(p_blocks, p_cols, l_blocks, l_cols, charges, currents, omegas, resist, branch_ends):
    n_blk, n_cell = lax.axis_size("blk"), lax.axis_size("cell")
    freq_count, _, share = charges.shape
    rows = 2 * freq_count
    reg_blocks = n_cell * share // 128
    vmem = pl.BlockSpec(memory_space=pltpu.VMEM)
    operands = (
        charges, currents, branch_ends, resist.reshape(1, share), omegas,
        p_cols.transpose(0, 2, 1), l_cols.transpose(0, 2, 1), p_blocks, l_blocks,
    )
    spaces = [pltpu.VMEM] * 4 + [pltpu.SMEM] * 3 + [pltpu.VMEM] * 2
    dma = pltpu.SemaphoreType.DMA
    outs = pl.pallas_call(
        functools.partial(kernel, n_blk, n_cell),
        out_shape=pltpu.VMEM((2, freq_count, 2, share), jnp.float32),
        in_specs=[pl.BlockSpec(memory_space=pltpu.HBM)] * len(operands),
        out_specs=vmem,
        scratch_shapes=[pltpu.VMEM((reg_blocks, rows, 128), jnp.bfloat16)] * n_blk
        + [pltpu.VMEM((reg_blocks, rows, 128), jnp.bfloat16)] * n_blk
        + [space(x.shape, x.dtype) for space, x in zip(spaces, operands)]
        + [
            pltpu.VMEM((n_cell * share, share), jnp.bfloat16),
            pltpu.VMEM((n_cell, rows, share), jnp.bfloat16),
            pltpu.VMEM((n_cell, rows, share), jnp.bfloat16),
            pltpu.VMEM((n_cell, rows, share), jnp.bfloat16),
            dma((len(operands),)),
            dma((n_blk, n_cell)), dma((n_blk, n_cell)),
            dma((n_blk, n_cell)), dma((n_blk, n_cell)),
            dma((n_cell,)), dma((n_cell,)),
            dma((n_cell,)), dma((n_cell,)),
        ],
        compiler_params=pltpu.CompilerParams(
            collective_id=0, has_side_effects=True, vmem_limit_bytes=60 * 2**20
        ),
    )(*[pltpu.with_memory_space_constraint(x, pltpu.HBM) for x in operands])
    return outs[0], outs[1]


def solution(mesh):
    across = ("job", "blk", "cell")
    placed = (
        P(across, None, None, None, None),
        P(across, None, None),
        P(across, None, None, None, None),
        P(across, None, None),
        P("col", None, across),
        P("col", None, across),
        P("col"),
        P(across),
        P(None, across),
    )
    return jax.shard_map(
        per_device,
        mesh=mesh,
        in_specs=placed,
        out_specs=(P("col", None, across), P("col", None, across)),
        check_vma=False,
    )
```

time: 26.1 us -> 18.9 us (0.72)
  local copies, waits for them, and re-layouts: 6.77 us -> 0.64 us
  Pallas kernels: 18.3 us -> 17.4 us
    unnamed x16 -> x0, local copies, waits for them, and re-layouts: 5.44 us -> none
    reshape x4 -> x0, local copies, waits for them, and re-layouts: 1.33 us -> none  [the longest x2 1.3 us: per_device(): return tuple((o.reshape(freq_count, 2, share) for o in outs))]
    pallas_call x1, Pallas kernels: 18.3 us -> 17.4 us  [per_device(): pl.pallas_call(functools.partial(kernel, n_blk, n_cell), out_shape=pltpu....]
    squeeze x0 -> x1, local copies, waits for them, and re-layouts: none -> 0.64 us  [per_device(): return (outs[0], outs[1])]
where the time goes in v2:
time: 18.9 us; the launch traced here: 18.7 us
  Pallas kernels  17.4 us (92%)
  local copies, waits for them, and re-layouts  0.64 us (3%)
  between operations  0.64 us (3%)
    pallas_call x1, Pallas kernels, per_device(): pl.pallas_call(functools.partial(kernel, n_blk, n_cell), out_shape=pltpu....  17.4 us
    squeeze x1, local copies, waits for them, and re-layouts, per_device(): return (outs[0], outs[1])  0.64 us

profile of v2, /device:TPU:0, one launch (start us, length us, event | category | flops | bytes accessed | tf_op | source)
XLA Modules:
  0.0 18.7 jit_solution(11793273310944169804)
XLA Ops:
  0.6 17.4 %shard_map.104 = f32[2,12,2,512]{3,2,1,0:T(2,128)S(1)} custom-call(bf16[12,2,512]{2,1,0:T(2,128)(2,1)} %refs_0_.1, bf16[12,2,512]{2,1,0:T(2,128)(2,1)} %refs_1_.1, s32[2,512]{1,0:T(2,128)} %refs_2_.1, f32[1,512]{1,0:T(1,128)} %bitcast.9, f32[12]{0:T(128)} %refs_4_.1, s32[4,2,4]{2,1,0:T(2,128)} %bitcast.7, s32[4,2,4]{2,1,0:T(2,128)} %bitcast.8, ...), custom_call_target="tpu_custom_call" | custom-call | tf_op jit(solution)/shard_map/pallas_call | solution.py:221
  18.1 0.6 %slice_bitcast_fusion = (f32[12,2,512]{2,1,0:T(2,128)}, f32[12,2,512]{2,1,0:T(2,128)}) fusion(f32[2,12,2,512]{3,2,1,0:T(2,128)S(1)} %shard_map.104), kind=kLoop, calls=%fused_computation | loop fusion | bytes 196608 | tf_op jit(solution)/shard_map/squeeze | solution.py:244

commit v3 on v2

--- a/solution.py
+++ b/solution.py
@@ -28,7 +28,7 @@
     a_bufs, b_bufs = scratch[:n_blk], scratch[n_blk : 2 * n_blk]
     targets = scratch[2 * n_blk : 2 * n_blk + 9]
     charges, currents, ends, resist, omegas, p_cols, l_cols, p_buf, l_buf = targets
-    (inc, phi, part_out, part_in, load_sem, a_send, a_recv, b_send, b_recv,
+    (acc, inc, phi, part_out, part_in, load_sem, a_send, a_recv, b_send, b_recv,
      phi_send, phi_recv, part_send, part_recv) = scratch[2 * n_blk + 9 :]
     rows, share = 2 * charges.shape[0], charges.shape[2]
     local = share // 128
@@ -79,13 +79,19 @@
         return send(group, d, c, False)
 
     order = sorted(range(1, n_blk), key=lambda d: min(d, n_blk - d))
+
+    def by_distance(distances, step, sending):
+        for dist in distances:
+            back, on = (n_blk - dist, dist) if sending else (dist, n_blk - dist)
+            pl.when(my_blk >= dist)(functools.partial(step, back))
+            pl.when(my_blk + dist < n_blk)(functools.partial(step, on))
+
     hops = range(1, n_cell)
     a_set, b_set = (a_bufs, a_send, a_recv), (b_bufs, b_send, b_recv)
     for group in (a_set, b_set):
-        for d in order[::-1]:
-            along_blk(group, d).start()
         for c in hops:
             along_cell(group, 0, c).start()
+        by_distance(range(n_blk - 1, 0, -1), lambda d: along_blk(group, d).start(), True)
     for load in loads[2:]:
         load.start()
 
@@ -117,12 +123,15 @@
     for c in hops:
         owner = lax.rem(my_cell + c, n_cell)
         part_out[c] = dot(i16, inc_of(owner), NT).astype(jnp.bfloat16)
+        part_copy(c).start()
 
     def pass_on(group):
-        for d in order:
+        def step(d):
             along_blk(group, d).wait_recv()
             for c in hops:
                 along_cell(group, d, c).start()
+
+        by_distance(range(1, n_blk), step, False)
 
     pass_on(a_set)
 
@@ -133,13 +142,16 @@
         omega = jnp.where(row == f, omegas[f], omega)
     omega = jnp.concatenate([omega] * local, axis=1)
 
-    def add_products(acc, blocks, cols, d, pick):
+    def add_products(acc, blocks, cols, pick, first, d):
         source = lax.rem(my_blk + n_blk - d, n_blk)
         for r in range(local):
             left = jnp.concatenate([pick(d, cols[r, k, source]) for k in range(2)], axis=1)
             right = jnp.concatenate([blocks[r, source, k] for k in range(2)], axis=1)
             term = dot(left, right, NT)
-            acc[r] = term if acc[r] is None else acc[r] + term
+            if first:
+                acc[r] = term
+            else:
+                acc[r] += term
 
     def pick_q(d, j):
         return a_bufs[d][j]
@@ -150,16 +162,18 @@
     for c in hops:
         along_cell(a_set, 0, c).wait_recv()
     loads[7].wait()
-    acc = [None] * local
-    add_products(acc, p_buf, p_cols, 0, pick_q)
+    add_products(acc, p_buf, p_cols, pick_q, True, 0)
 
     pass_on(b_set)
-    for d in order:
+
+    def arrive_a(d):
         for c in hops:
             along_cell(a_set, d, c).wait_recv()
-        add_products(acc, p_buf, p_cols, d, pick_q)
-
-    phi[0] = jnp.concatenate(acc, axis=1).astype(jnp.bfloat16)
+        add_products(acc, p_buf, p_cols, pick_q, False, d)
+
+    by_distance(range(1, n_blk), arrive_a, False)
+
+    phi[0] = jnp.concatenate([acc[r] for r in range(local)], axis=1).astype(jnp.bfloat16)
 
     def phi_copy(c):
         return pltpu.make_async_remote_copy(
@@ -169,19 +183,19 @@
 
     for c in hops:
         phi_copy(c).start()
-    for c in hops:
-        part_copy(c).start()
 
     for c in hops:
         along_cell(b_set, 0, c).wait_recv()
     loads[8].wait()
-    acc = [None] * local
-    add_products(acc, l_buf, l_cols, 0, pick_i)
-    for d in order:
+    add_products(acc, l_buf, l_cols, pick_i, True, 0)
+
+    def arrive_b(d):
         for c in hops:
             along_cell(b_set, d, c).wait_recv()
-        add_products(acc, l_buf, l_cols, d, pick_i)
-    flux = jnp.concatenate(acc, axis=1)
+        add_products(acc, l_buf, l_cols, pick_i, False, d)
+
+    by_distance(range(1, n_blk), arrive_b, False)
+    flux = jnp.concatenate([acc[r] for r in range(local)], axis=1)
     cell = resist[...] * i32 + omega * quarter_turn(flux)
     drop = dot(phi[0], inc_of(my_cell), NN)
 
@@ -227,6 +241,7 @@
         + [pltpu.VMEM((reg_blocks, rows, 128), jnp.bfloat16)] * n_blk
         + [space(x.shape, x.dtype) for space, x in zip(spaces, operands)]
         + [
+            pltpu.VMEM((share // 128, rows, 128), jnp.float32),
             pltpu.VMEM((n_cell * share, share), jnp.bfloat16),
             pltpu.VMEM((n_cell, rows, share), jnp.bfloat16),
             pltpu.VMEM((n_cell, rows, share), jnp.bfloat16),

time: 18.9 us -> 17.1 us (0.905)
  Pallas kernels: 17.4 us -> 15.6 us
    pallas_call x1, Pallas kernels: 17.4 us -> 15.6 us  [per_device(): pl.pallas_call(functools.partial(kernel, n_blk, n_cell), out_shape=pltpu....]
where the time goes in v3:
time: 17.1 us; the launch traced here: 16.9 us
  Pallas kernels  15.6 us (91%)
  local copies, waits for them, and re-layouts  0.64 us (4%)
  between operations  0.64 us (4%)
    pallas_call x1, Pallas kernels, per_device(): pl.pallas_call(functools.partial(kernel, n_blk, n_cell), out_shape=pltpu....  15.6 us
    squeeze x1, local copies, waits for them, and re-layouts, per_device(): return (outs[0], outs[1])  0.64 us

profile of v3, /device:TPU:0, one launch (start us, length us, event | category | flops | bytes accessed | tf_op | source)
XLA Modules:
  0.0 16.9 jit_solution(6891383924228835387)
XLA Ops:
  0.6 15.6 %shard_map.104 = f32[2,12,2,512]{3,2,1,0:T(2,128)S(1)} custom-call(bf16[12,2,512]{2,1,0:T(2,128)(2,1)} %refs_0_.1, bf16[12,2,512]{2,1,0:T(2,128)(2,1)} %refs_1_.1, s32[2,512]{1,0:T(2,128)} %refs_2_.1, f32[1,512]{1,0:T(1,128)} %bitcast.9, f32[12]{0:T(128)} %refs_4_.1, s32[4,2,4]{2,1,0:T(2,128)} %bitcast.7, s32[4,2,4]{2,1,0:T(2,128)} %bitcast.8, ...), custom_call_target="tpu_custom_call" | custom-call | tf_op jit(solution)/shard_map/pallas_call | solution.py:235
  16.3 0.6 %slice_bitcast_fusion = (f32[12,2,512]{2,1,0:T(2,128)}, f32[12,2,512]{2,1,0:T(2,128)}) fusion(f32[2,12,2,512]{3,2,1,0:T(2,128)S(1)} %shard_map.104), kind=kLoop, calls=%fused_computation | loop fusion | bytes 196608 | tf_op jit(solution)/shard_map/squeeze | solution.py:259

commit v4 on v3

--- a/solution.py
+++ b/solution.py
@@ -184,6 +184,12 @@
     for c in hops:
         phi_copy(c).start()
 
+    drop = dot(phi[0], inc_of(my_cell), NN)
+    for c in hops:
+        part_copy(c).wait_recv()
+        outflow += part_in[c].astype(jnp.float32)
+    panel_out[...] = (outflow + omega * quarter_turn(q32)).reshape(panel_out.shape)
+
     for c in hops:
         along_cell(b_set, 0, c).wait_recv()
     loads[8].wait()
@@ -197,12 +203,7 @@
     by_distance(range(1, n_blk), arrive_b, False)
     flux = jnp.concatenate([acc[r] for r in range(local)], axis=1)
     cell = resist[...] * i32 + omega * quarter_turn(flux)
-    drop = dot(phi[0], inc_of(my_cell), NN)
-
-    for c in hops:
-        part_copy(c).wait_recv()
-        outflow += part_in[c].astype(jnp.float32)
-    panel_out[...] = (outflow + omega * quarter_turn(q32)).reshape(panel_out.shape)
+
 
     for c in hops:
         phi_copy(c).wait_recv()

time: 17.1 us -> 17.1 us (level)
  no operation moved by 1% of the time
where the time goes in v4:
time: 17.1 us; the launch traced here: 16.9 us
  Pallas kernels  15.6 us (91%)
  local copies, waits for them, and re-layouts  0.64 us (4%)
  between operations  0.64 us (4%)
    pallas_call x1, Pallas kernels, per_device(): pl.pallas_call(functools.partial(kernel, n_blk, n_cell), out_shape=pltpu....  15.6 us
    squeeze x1, local copies, waits for them, and re-layouts, per_device(): return (outs[0], outs[1])  0.64 us

profile of v4, /device:TPU:0, one launch (start us, length us, event | category | flops | bytes accessed | tf_op | source)
XLA Modules:
  0.0 16.9 jit_solution(16531000278123048981)
XLA Ops:
  0.6 15.6 %shard_map.104 = f32[2,12,2,512]{3,2,1,0:T(2,128)S(1)} custom-call(bf16[12,2,512]{2,1,0:T(2,128)(2,1)} %refs_0_.1, bf16[12,2,512]{2,1,0:T(2,128)(2,1)} %refs_1_.1, s32[2,512]{1,0:T(2,128)} %refs_2_.1, f32[1,512]{1,0:T(1,128)} %bitcast.9, f32[12]{0:T(128)} %refs_4_.1, s32[4,2,4]{2,1,0:T(2,128)} %bitcast.7, s32[4,2,4]{2,1,0:T(2,128)} %bitcast.8, ...), custom_call_target="tpu_custom_call" | custom-call | tf_op jit(solution)/shard_map/pallas_call | solution.py:236
  16.3 0.6 %slice_bitcast_fusion = (f32[12,2,512]{2,1,0:T(2,128)}, f32[12,2,512]{2,1,0:T(2,128)}) fusion(f32[2,12,2,512]{3,2,1,0:T(2,128)S(1)} %shard_map.104), kind=kLoop, calls=%fused_computation | loop fusion | bytes 196608 | tf_op jit(solution)/shard_map/squeeze | solution.py:260
